TPU v7x, 32 devices: a whole 2x2x4 slice. The times are simulated.
32 devices in a mesh: dp: 8 (over y, x, core), tensor: 4 (over z).
Axes of the slice: x: 2, y: 2, z: 4, core: 2. Of those that a mesh axis runs over, the one named last changes fastest.
Arguments:
- inputs: bfloat16 [16384, 768], P('dp'), may hold values from -6 to 6
- cotangent: bfloat16 [16384, 768], P('dp'), may hold values from -6 to 6
- counts: int32 [32], P('dp'), may hold values from 40 to 512, as said below
- keep_mask: int32 [16384], P('dp'), may hold values 0 or 1
- box_x: int32 [16384], P('dp'), may hold values from 0 to 63
- box_y: int32 [16384], P('dp'), may hold values from 0 to 63
- gain_one: float32 [768], replicated, may hold values from 0.5 to 1.5
- shift_one: float32 [768], replicated, may hold values from -4 to 4
- w_qkv: bfloat16 [3, 768, 768], P(None, None, 'tensor'), may hold values from -0.21875 to 0.21875
- b_qv: float32 [2, 768], P(None, 'tensor'), may hold values from -4 to 4
- w_out: bfloat16 [768, 768], P('tensor'), may hold values from -0.875 to 0.875
- b_out: float32 [768], replicated, may hold values from -4 to 4
- gain_two: float32 [768], replicated, may hold values from 0.5 to 1.5
- shift_two: float32 [768], replicated, may hold values from -4 to 4
- w_up: bfloat16 [768, 3072], P(None, 'tensor'), may hold values from -0.21875 to 0.21875
- b_up: float32 [3072], P('tensor'), may hold values from -4 to 4
- w_down: bfloat16 [3072, 768], P('tensor'), may hold values from -0.109375 to 0.109375
- b_down: float32 [768], replicated, may hold values from -4 to 4
- rel_tables: float32 [2, 12, 64], P(None, 'tensor'), may hold values from -4 to 4
Outputs:
- out: bfloat16 [16384, 768], P('dp')
- grad_input: bfloat16 [16384, 768], P('dp')
- grad_w_qkv: float32 [3, 768, 768], P(None, None, 'tensor')
- grad_b_qv: float32 [2, 768], P(None, 'tensor')
- grad_w_out: float32 [768, 768], P('tensor')
- grad_b_out: float32 [768], replicated
- grad_gain_one: float32 [768], replicated
- grad_shift_one: float32 [768], replicated
- grad_gain_two: float32 [768], replicated
- grad_shift_two: float32 [768], replicated
- grad_w_up: float32 [768, 3072], P(None, 'tensor')
- grad_b_up: float32 [3072], P('tensor')
- grad_w_down: float32 [3072, 768], P('tensor')
- grad_b_down: float32 [768], replicated
- grad_tables: float32 [2, 12, 64], P(None, 'tensor')
Inputs may be any that keep to these rules, and one draw needn't show every extreme that they name: The first counts[p] slots of page p hold tokens and the rest are padding; in every draw some page has all 512 slots in use.
All inputs are finite; a program needn't handle non-finite values. No bound on the sum of `keep_mask` on one device may be relied on, other than what follows from the above.
Results may differ from a plain program's by a relative error of at most 0.017.
Values may be sent and summed in bfloat16 or wider, within the bound.
A program may use at most 128 MiB of HBM per device.

v0:
```python
import jax
import jax.numpy as jnp
from jax import lax
from jax.sharding import PartitionSpec as P

HEAD_DIM = 64
PAGE = 512


epsilon = 1e-05
masked_score = -1e30
exact_precision = lax.Precision.HIGHEST


def normalize(values, scale_vec, shift_vec):
    average = jnp.mean(values, axis=-1, keepdims=True)
    centered = values - average
    variance = jnp.mean(centered * centered, axis=-1, keepdims=True)
    return centered * lax.rsqrt(variance + epsilon) * scale_vec + shift_vec


def gelu_pair(upper_in):
    cumulative = 0.5 * (1.0 + lax.erf(upper_in * 0.7071067811865476))
    density = jnp.exp(-0.5 * upper_in * upper_in) * 0.3989422804014327
    return (upper_in * cumulative, cumulative + upper_in * density)


def selector(bins):
    half_bins = bins // 2
    levels = jnp.arange(bins, dtype=jnp.int32)
    offsets = jnp.clip(levels[None, :] - levels[:, None], -half_bins, half_bins - 1) + half_bins
    return (offsets[:, :, None] == levels[None, None, :]).astype(jnp.float32)


def one_hot_rows(box_page, bins):
    levels = jnp.arange(bins, dtype=jnp.int32)
    return (box_page[:, None] == levels[None, :]).astype(jnp.float32)


def spread_table(table, selected_buckets, select):
    squared_values = jnp.einsum("hc,abc->hab", table, select, precision=exact_precision)
    remaining_tokens = jnp.einsum(
        "gw,kwz->kgz", selected_buckets, squared_values, precision=exact_precision
    )
    return jnp.einsum("ytg,fg->ytf", remaining_tokens, selected_buckets, precision=exact_precision)


def page_bias(tables, page_box_x, page_box_y, select):
    bins = tables.shape[-1]
    picks_x = one_hot_rows(page_box_x, bins)
    picks_y = one_hot_rows(page_box_y, bins)
    return spread_table(tables[0], picks_x, select) + spread_table(tables[1], picks_y, select)


def fold_table(grad_scores, selected_buckets, select):
    remaining_tokens = jnp.einsum(
        "ia,hij->haj", selected_buckets, grad_scores, precision=exact_precision
    )
    squared_values = jnp.einsum(
        "haj,jb->hab", remaining_tokens, selected_buckets, precision=exact_precision
    )
    return jnp.einsum("hab,abc->hc", squared_values, select, precision=exact_precision)


def table_grad(grad_scores, page_box_x, page_box_y, select):
    bins = select.shape[0]
    picks_x = one_hot_rows(page_box_x, bins)
    picks_y = one_hot_rows(page_box_y, bins)
    return jnp.stack(
        [fold_table(grad_scores, picks_x, select), fold_table(grad_scores, picks_y, select)]
    )


def allowed_mask(page_count, keep_page):
    positions = jnp.arange(keep_page.shape[0], dtype=jnp.int32)
    return (positions[None, :] == positions[:, None]) | (positions[None, :] < page_count) & (
        keep_page[None, :] == 1
    )


def on_device(
    inputs,
    cotangent,
    counts,
    keep_mask,
    box_x,
    box_y,
    gain_one,
    shift_one,
    w_qkv,
    b_qv,
    w_out,
    b_out,
    gain_two,
    shift_two,
    w_up,
    b_up,
    w_down,
    b_down,
    rel_tables,
):
    page_len = PAGE
    tok_rows = inputs.shape[0]
    pages_here = tok_rows // page_len
    heads_here = rel_tables.shape[1]
    bins = rel_tables.shape[-1]
    select = selector(bins)
    attention_score_scale = HEAD_DIM ** (-0.5)
    positions = jnp.arange(page_len, dtype=jnp.int32)
    validity = (positions[None, :] < counts[:, None]).astype(jnp.float32).reshape(tok_rows, 1)
    tokens = inputs.astype(jnp.float32)
    normed_one, pull_one = jax.vjp(normalize, tokens, gain_one, shift_one)
    low_one = normed_one.astype(jnp.bfloat16)
    projected = jnp.einsum("td,sde->tse", low_one, w_qkv, preferred_element_type=jnp.float32)
    queries = (projected[:, 0] + b_qv[0]).astype(jnp.bfloat16)
    key_rows = projected[:, 1].astype(jnp.bfloat16)
    values = (projected[:, 2] + b_qv[1]).astype(jnp.bfloat16)

    def paged(array):
        return array.reshape(pages_here, page_len, heads_here, HEAD_DIM)

    page_meta = (
        counts,
        keep_mask.reshape(pages_here, page_len),
        box_x.reshape(pages_here, page_len),
        box_y.reshape(pages_here, page_len),
    )

    def scores_of(query_page, key_page, bias_page, allowed):
        raw = (
            jnp.einsum("ihe,jhe->hij", query_page, key_page, preferred_element_type=jnp.float32)
            * attention_score_scale
            + bias_page
        )
        return jnp.where(allowed[None], raw, masked_score)

    def page_forward(pieces):
        query_page, key_page, value_page, page_count, keep_page, page_box_x, page_box_y = pieces
        bias_page = page_bias(rel_tables, page_box_x, page_box_y, select)
        scores = scores_of(query_page, key_page, bias_page, allowed_mask(page_count, keep_page))
        top_score = jnp.max(scores, axis=-1, keepdims=True)
        shifted = jnp.exp(scores - top_score)
        total = jnp.sum(shifted, axis=-1, keepdims=True)
        probs_low = (shifted / total).astype(jnp.bfloat16)
        context_page = jnp.einsum(
            "hij,jhe->ihe", probs_low, value_page, preferred_element_type=jnp.float32
        )
        return (context_page.astype(jnp.bfloat16), top_score + jnp.log(total), bias_page)

    context, log_totals, biases = lax.map(
        page_forward, (paged(queries), paged(key_rows), paged(values)) + page_meta
    )
    context = context.reshape(tok_rows, -1)
    attn_part = jnp.dot(context, w_out, preferred_element_type=jnp.float32)
    attended = lax.psum(attn_part, "tensor")
    hidden = tokens + attended + b_out
    normed_two, pull_two = jax.vjp(normalize, hidden, gain_two, shift_two)
    low_two = normed_two.astype(jnp.bfloat16)
    up_proj = jnp.dot(low_two, w_up, preferred_element_type=jnp.float32) + b_up
    activated, slope = gelu_pair(up_proj)
    act_low = activated.astype(jnp.bfloat16)
    down_part = jnp.dot(act_low, w_down, preferred_element_type=jnp.float32)
    down_proj = lax.psum(down_part.astype(jnp.bfloat16), "tensor").astype(jnp.float32)
    result = validity * (hidden + down_proj + b_down)
    grad_result = validity * cotangent.astype(jnp.float32)
    grad_b_down = jnp.sum(grad_result, axis=0)
    grad_down = grad_result.astype(jnp.bfloat16)
    grad_w_down = jnp.einsum("tf,td->fd", act_low, grad_down, preferred_element_type=jnp.float32)
    grad_act = jnp.einsum("td,fd->tf", grad_down, w_down, preferred_element_type=jnp.float32)
    grad_up = (grad_act * slope).astype(jnp.bfloat16)
    grad_b_up = jnp.sum(grad_up.astype(jnp.float32), axis=0)
    grad_w_up = jnp.einsum("td,tf->df", low_two, grad_up, preferred_element_type=jnp.float32)
    grad_normed_part = jnp.einsum("tf,df->td", grad_up, w_up, preferred_element_type=jnp.float32)
    grad_normed_two = lax.psum(grad_normed_part, "tensor")
    hidden_norm_gradient, grad_gain_two, grad_shift_two = pull_two(grad_normed_two)
    grad_hidden = grad_result + hidden_norm_gradient
    mlp_summed = (grad_w_up, grad_b_up, grad_w_down, grad_b_down, grad_gain_two, grad_shift_two)
    grad_b_out = jnp.sum(grad_hidden, axis=0)
    grad_attended = grad_hidden.astype(jnp.bfloat16)
    grad_w_out = jnp.einsum("te,td->ed", context, grad_attended, preferred_element_type=jnp.float32)
    grad_context = jnp.einsum(
        "td,ed->te", grad_attended, w_out, preferred_element_type=jnp.float32
    ).astype(jnp.bfloat16)

    def page_backward(pieces):
        (
            query_page,
            key_page,
            value_page,
            page_count,
            keep_page,
            page_box_x,
            page_box_y,
            bias_page,
            log_page,
            grad_page,
        ) = pieces
        scores = scores_of(query_page, key_page, bias_page, allowed_mask(page_count, keep_page))
        probs = jnp.exp(scores - log_page)
        probs_low = probs.astype(jnp.bfloat16)
        grad_value_page = jnp.einsum(
            "hij,ihe->jhe", probs_low, grad_page, preferred_element_type=jnp.float32
        )
        grad_probs = jnp.einsum(
            "ihe,jhe->hij", grad_page, value_page, preferred_element_type=jnp.float32
        )
        row_delta = jnp.sum(probs * grad_probs, axis=-1, keepdims=True)
        grad_scores = probs * (grad_probs - row_delta)
        grad_low = grad_scores.astype(jnp.bfloat16)
        grad_query_page = (
            jnp.einsum("hij,jhe->ihe", grad_low, key_page, preferred_element_type=jnp.float32)
            * attention_score_scale
        )
        grad_key_page = (
            jnp.einsum("hij,ihe->jhe", grad_low, query_page, preferred_element_type=jnp.float32)
            * attention_score_scale
        )
        table_part = table_grad(grad_scores, page_box_x, page_box_y, select)
        return (
            grad_query_page.astype(jnp.bfloat16),
            grad_key_page.astype(jnp.bfloat16),
            grad_value_page.astype(jnp.bfloat16),
            table_part,
        )

    query_gradient_rows, grad_keys, grad_values, table_parts = lax.map(
        page_backward,
        (paged(queries), paged(key_rows), paged(values))
        + page_meta
        + (biases, log_totals, paged(grad_context)),
    )
    grad_tables = jnp.sum(table_parts, axis=0)
    query_gradient_rows = query_gradient_rows.reshape(tok_rows, -1)
    grad_keys = grad_keys.reshape(tok_rows, -1)
    grad_values = grad_values.reshape(tok_rows, -1)
    grad_proj = jnp.stack([query_gradient_rows, grad_keys, grad_values], axis=1)
    grad_b_qv = jnp.stack(
        [
            jnp.sum(query_gradient_rows.astype(jnp.float32), axis=0),
            jnp.sum(grad_values.astype(jnp.float32), axis=0),
        ]
    )
    grad_w_qkv = jnp.einsum("td,tse->sde", low_one, grad_proj, preferred_element_type=jnp.float32)
    grad_normed_local = jnp.einsum(
        "tse,sde->td", grad_proj, w_qkv, preferred_element_type=jnp.float32
    )
    grad_normed_one = lax.psum(grad_normed_local.astype(jnp.bfloat16), "tensor").astype(jnp.float32)
    grad_tokens_norm, grad_gain_one, grad_shift_one = pull_one(grad_normed_one)
    grad_input = (grad_hidden + grad_tokens_norm).astype(jnp.bfloat16)
    out_low = result.astype(jnp.bfloat16)
    summed_all = lax.psum(
        (
            grad_w_qkv,
            grad_b_qv,
            grad_w_out,
            grad_b_out,
            grad_gain_one,
            grad_shift_one,
            grad_tables,
            grad_w_up,
            grad_b_up,
            grad_w_down,
            grad_b_down,
            grad_gain_two,
            grad_shift_two,
        ),
        "dp",
    )
    attn_summed = summed_all[:7]
    mlp_summed = summed_all[7:]
    return (
        out_low,
        grad_input,
        attn_summed[0],
        attn_summed[1],
        attn_summed[2],
        attn_summed[3],
        attn_summed[4],
        attn_summed[5],
        mlp_summed[4],
        mlp_summed[5],
        mlp_summed[0],
        mlp_summed[1],
        mlp_summed[2],
        mlp_summed[3],
        attn_summed[6],
    )


def solution(mesh):
    placed = (
        P("dp", None),
        P("dp", None),
        P("dp"),
        P("dp"),
        P("dp"),
        P("dp"),
        P(),
        P(),
        P(None, None, "tensor"),
        P(None, "tensor"),
        P("tensor", None),
        P(),
        P(),
        P(),
        P(None, "tensor"),
        P("tensor"),
        P("tensor", None),
        P(),
        P(None, "tensor", None),
    )
    return jax.shard_map(
        on_device,
        mesh=mesh,
        in_specs=placed,
        out_specs=(
            P("dp", None),
            P("dp", None),
            P(None, None, "tensor"),
            P(None, "tensor"),
            P("tensor", None),
            P(),
            P(),
            P(),
            P(),
            P(),
            P(None, "tensor"),
            P("tensor"),
            P("tensor", None),
            P(),
            P(None, "tensor", None),
        ),
        check_vma=False,
    )
```

profile of v0, /device:TPU:0, one launch (start us, length us, event | category | flops | bytes accessed | tf_op | source)
XLA Modules:
  0.0 1052.8 jit_solution(11376313114288689183)
XLA Ops:
  21.8 4.3 fusion.134
  27.7 4.2 fusion.133
  45.5 53.5 %while.34 = (s32[]{:T(128)}, bf16[4,512,3,64]{1,3,2,0:T(8,128)(2,1)}, f32[4,3,512,1]{2,1,3,0:T(4,128)}, f32[4,3,512,512]{2,3,1,0:T(8,128)}, bf16[4,512,3,64]{1,3...) while((s32[]{:T(128)}, ...), condition=%wide.region_5.6_spmd, body=%wide.region_2.5_spmd.sunk | while | flops 1568899072 | bytes 28224684 | solution.py:150
  106.3 224.4 %all-reduce.8.cloned.1.call-done = f32[2048,768]{1,0:T(8,128)} async-done(((f32[2048,768]{1,0:T(8,128)}), f32[2048,768]{1,0:T(8,128)}) %all-reduce.8.cloned.1.call-update) | async-done | bytes 6291472 | tf_op jit(solution)/shard_map/psum | solution.py:155
  330.7 4.6 fusion.144
  339.2 5.2 multiply_convert_fusion.1
  344.4 5.9 convert_reduce_fusion.2
  352.1 4.6 fusion.150
  356.8 6.5 convolution_convert_fusion
  363.3 215.4 %all-reduce.10.cloned.1.call-done = f32[2048,768]{1,0:T(8,128)} async-done(((f32[2048,768]{1,0:T(8,128)}), f32[2048,768]{1,0:T(8,128)}) %all-reduce.10.cloned.1.call-update) | async-done | bytes 6291472 | tf_op jit(solution)/shard_map/psum | solution.py:174
  578.7 6.4 multiply_reduce_fusion.1
  585.2 4.4 fusion.143
  601.3 79.9 %while.35 = (s32[]{:T(128)}, bf16[4,512,3,64]{1,3,2,0:T(8,128)(2,1)}, bf16[4,512,3,64]{1,3,2,0:T(8,128)(2,1)}, bf16[4,512,3,64]{1,3,2,0:T(8,128)(2,1)}, f32[4,2,...) while((s32[]{:T(128)}, ...), condition=%wide.region_15.16_spmd.clone.clone, body=%wide.region_13.15_spmd.clone.clone.sunk | while | flops 1891991936 | bytes 42174788 | solution.py:226
  694.9 4.0 bitcast_convert_fusion
  699.0 7.1 fusion.151
  706.1 4.3 fusion.130
  710.7 4.5 fusion.124
  719.3 202.0 %all-reduce.14.cloned.1.call-done = (bf16[2048,768]{1,0:T(8,128)(2,1)}, bf16[2048,768]{1,0:T(8,128)(2,1)}) async-done(((bf16[2048,768]{1,0:T(8,128)(2,1)}, bf16[2048,768]{1,0:T(8,128)(2,1)}), (bf16[2048,768]{1,0:T(8,128)(2,1)}, bf16[2048,768]{1,0:T(8,128)(2,1)})) %all-reduce.14.cloned.1.call-update) | async-done | bytes 6291472 | tf_op jit(solution)/shard_map/psum | solution.py:163
  921.3 4.8 convert_reduce_fusion
  926.2 3.7 fusion.114
  930.0 27.2 %all-reduce = (f32[2,192]{1,0:T(2,128)}, f32[768]{0:T(1024)}, f32[768]{0:T(1024)}, f32[768]{0:T(1024)}, f32[768]{0:T(1024)}, /*index=5*/f32[768]{0:T(1024)}, f32...) all-reduce(f32[2,192]{1,0:T(2,128)S(1)} %pad_maximum_fusion, ...), channel_id=1, replica_groups=mesh['dp'=8,'tensor'=4] {'dp'}, use_global_device_ids=true, to_apply=%region_22.23 | all-reduce | flops 6144 | bytes 49152 | tf_op jit(solution)/shard_map/psum | solution.py:251
  957.8 5.7 multiply_convert_fusion
  966.1 3.7 add_convert_fusion
  969.8 69.7 %all-reduce.12.cloned.1.call-done = (f32[3,768,192]{1,2,0:T(8,128)}, f32[192,768]{1,0:T(8,128)}, f32[768,768]{1,0:T(8,128)}, f32[768,768]{1,0:T(8,128)}) async-done(((f32[3,768,192]{1,2,0:T(8,128)}, f32[192,768]{1,0:T(8,128)}, f32[768,768]{1,0:T(8,128)}, f32[768,768]{1,0:T(8,128)}), (f32[3,768,192]{1,2,0:T(8,128)}, f32[192,768]{1,0:T(8,128)}, f32[768,768]{1,0:T(8,128)}, ...) | async-done | bytes 7077904 | tf_op jit(solution)/shard_map/psum | solution.py:251
  (342 shorter events, 214.3 us)
Async XLA Ops:
  7.2 331.9 %copy-start = (bf16[768,768]{1,0:T(8,128)(2,1)S(1)}, bf16[768,768]{1,0:T(8,128)(2,1)}, u32[]{:S(2)}) copy-start(bf16[768,768]{1,0:T(8,128)(2,1)} %param.37) | copy-start | bytes 3538948
  7.2 323.5 %all-reduce.8.cloned.1.call-start = ((), (), s32[]{:S(2)}) async-start(), calls=%async_computation | async-start | bytes 12582912 | tf_op jit(solution)/shard_map/psum | solution.py:155
  99.0 5.9 copy-start.28
  99.0 5.9 copy-start.29
  105.0 225.7 %copy-start.53 = (f32[768]{0:T(1024)S(1)}, f32[768]{0:T(1024)}, u32[]{:S(2)}) copy-start(f32[768]{0:T(1024)} %param.34) | copy-start | bytes 9220
  105.0 473.7 %all-reduce.10.cloned.1.call-start = ((), (), s32[]{:S(2)}) async-start(), calls=%async_computation.1 | async-start | bytes 12582912 | tf_op jit(solution)/shard_map/psum | solution.py:174
  339.1 5.2 copy-start.18
  339.1 5.2 copy-start.15
  339.2 5.2 copy-start.32
  356.7 564.6 %all-reduce.14.cloned.1.call-start = ((), (), s32[]{:S(2)}) async-start(), calls=%async_computation.3 | async-start | bytes 12582912 | tf_op jit(solution)/shard_map/psum | solution.py:163
  356.7 221.9 %copy-start.42 = (f32[768]{0:T(1024)S(1)}, f32[768]{0:T(1024)}, u32[]{:S(2)}) copy-start(f32[768]{0:T(1024)} %param.35) | copy-start | bytes 9220
  363.3 221.8 %copy-start.38 = (f32[2048]{0:T(1024)S(1)}, f32[2048]{0:T(1024)}, u32[]{:S(2)}) copy-start(f32[2048]{0:T(1024)} %copy-done.37) | copy-start | bytes 24580
  578.7 6.5 copy-start.10
  595.7 5.6 copy-start.46
  681.3 7.2 copy-start.14
  699.0 7.1 copy-start.34
  699.0 340.5 %all-reduce.12.cloned.1.call-start = ((), (), s32[]{:S(2)}) async-start(), calls=%async_computation.2 | async-start | bytes 14155776 | tf_op jit(solution)/shard_map/psum | solution.py:251
  699.0 7.1 copy-start.17
  699.0 7.1 copy-start.63
  926.2 31.6 %copy-start.50 = (f32[768]{0:T(1024)S(1)}, f32[768]{0:T(1024)}, u32[]{:S(2)}) copy-start(f32[768]{0:T(1024)} %param.40) | copy-start | bytes 9220
  926.2 37.4 %slice-start = ((s8[6291456]{0:T(1024)(128)(4,1)}), s8[2097152]{0:T(1024)(128)(4,1)S(1)}, s32[]{:S(2)}) async-start(s8[6291456]{0:T(1024)(128)(4,1)} %bitcast.286), calls=%async_computation.4 | async-start | bytes 4194304
  957.8 5.7 copy-start.6
  957.8 7.4 slice-start.1
  957.8 8.2 copy-start.9
  (53 other events, 179.5 us)
Sparse Core Ops, SparseCore 0:
  105.1 225.5 all-reduce.7
  356.8 221.7 all-reduce.9
  699.1 222.1 all-reduce.13
  926.0 113.4 all-reduce.11
where the time goes:
time: 1060 us; the launch traced here: 1050 us
  waiting for transfers between devices  712 us (67%)
  matrix products  161 us (15%)
  local copies, waits for them, and re-layouts  74.7 us (7%)
  other arithmetic  62.3 us (6%)
  blocking collectives  27.2 us (3%)
  between operations  14.8 us (1%)
    psum x1, waiting for transfers between devices, on_device(): attended = lax.psum(attn_part, 'tensor')  224 us
    psum x1, waiting for transfers between devices, on_device(): grad_normed_two = lax.psum(grad_normed_part, 'tensor')  215 us
    psum x1, waiting for transfers between devices, on_device(): lax.psum(down_part.astype(jnp.bfloat16), 'tensor').astype(jnp.float32)  202 us
    psum x1, waiting for transfers between devices, on_device(): lax.psum((grad_w_qkv, grad_b_qv, grad_w_out, grad_b_out, grad_gain_one, g...  69.7 us
    psum x1, blocking collectives, on_device(): lax.psum((grad_w_qkv, grad_b_qv, grad_w_out, grad_b_out, grad_gain_one, g...  27.2 us
    unnamed x140, local copies, waits for them, and re-layouts  22.3 us
  transfers between devices with their start and end apart: 4, of which 4 were waited for; matrix products, arithmetic and copies ran while one was open for 4% of the time, Pallas kernels for 0%

commit v1 on v0

v1 whole, which is shorter than its diff:
```python
import functools
import jax
import jax.numpy as jnp
from jax import lax
from jax.experimental import pallas as pl
from jax.experimental.pallas import tpu as pltpu
from jax.sharding import PartitionSpec as P

HEAD_DIM = 64
PAGE = 512
BLOCK = 128
epsilon = 1e-05
masked_score = -1e30
LOG2E = 1.4426950408889634
LN2 = 0.6931471805599453
bf16 = jnp.bfloat16
f32 = jnp.float32
VMEM_LIMIT = 60 << 20


def dot(left, right, left_dim, right_dim):
    return lax.dot_general(
        left, right, (((left_dim,), (right_dim,)), ((), ())), preferred_element_type=f32
    )


def nn(left, right):
    return dot(left, right, 1, 0)


def nt(left, right):
    return dot(left, right, 1, 1)


def tn(left, right):
    return dot(left, right, 0, 0)


def norm_parts(rows):
    average = jnp.mean(rows, axis=-1, keepdims=True)
    centered = rows - average
    variance = jnp.mean(centered * centered, axis=-1, keepdims=True)
    inverse = lax.rsqrt(variance + epsilon)
    return centered * inverse, inverse


def norm_grad(grad_out, xhat, inverse, gain):
    scaled = grad_out * gain
    mean_one = jnp.mean(scaled, axis=-1, keepdims=True)
    mean_two = jnp.mean(scaled * xhat, axis=-1, keepdims=True)
    return inverse * (scaled - mean_one - xhat * mean_two)


def one_hot_columns(meta_ref, width, bins):
    levels = lax.broadcasted_iota(jnp.int32, (bins, width), 0)
    hot_x = jnp.where(levels == meta_ref[0, 1:2, 0:width], 1.0, 0.0)
    hot_y = jnp.where(levels == meta_ref[0, 2:3, 0:width], 1.0, 0.0)
    return jnp.concatenate([hot_x, hot_y], axis=0).astype(bf16)


def by_blocks(count, most, body):
    blocks = (count + (BLOCK - 1)) // BLOCK
    for used in range(1, most + 1):
        pl.when(blocks == used)(functools.partial(body, used * BLOCK))


def forward_kernel(
    counts_ref,
    x_ref,
    meta_ref,
    rows_ref,
    bias_ref,
    toeplitz_ref,
    gathered_ref,
    qkv_ref,
    probs_ref,
    inverse_ref,
    context_ref,
    hidden_ref,
    weights,
    copy_sem,
    spread,
    scores,
):
    page = pl.program_id(0)
    width_model = x_ref.shape[1]
    heads = toeplitz_ref.shape[0] // 128
    bins = 64

    @pl.when(page == 0)
    def _():
        copies = [
            pltpu.make_async_copy(gathered_ref.at[:, kind], weights.at[kind], copy_sem.at[kind])
            for kind in range(4)
        ]
        for copy in copies:
            copy.start()
        for copy in copies:
            copy.wait()

    count = counts_ref[page]

    def body(width):
        tokens = x_ref[0:width, :].astype(f32)
        xhat, _ = norm_parts(tokens)
        low = (xhat * rows_ref[0:1, :] + rows_ref[1:2, :]).astype(bf16)
        for kind in range(3):
            weight = weights[kind].reshape(width_model, width_model)
            product = nt(weight, low)
            if kind == 0:
                product = (product + bias_ref[:, 0:1]) * (LOG2E * HEAD_DIM**-0.5)
            if kind == 2:
                product = product + bias_ref[:, 1:2]
            qkv_ref[0, kind, :, 0:width] = product.astype(bf16)
        hot = one_hot_columns(meta_ref, width, bins)
        spread[:, 0:width] = nn(toeplitz_ref[...], hot).astype(bf16)
        lane = lax.broadcasted_iota(jnp.int32, (1, width), 1)
        open_key = (lane < count) & (meta_ref[0, 0:1, 0:width] == 1)
        mask_row = jnp.where(open_key, 0.0, masked_score)
        first = lax.broadcasted_iota(jnp.int32, (HEAD_DIM, width), 0) == 0
        key_pad = jnp.where(first, mask_row, 0.0).astype(bf16)
        query_pad = jnp.where(first, 1.0, 0.0).astype(bf16)
        ones = jnp.ones((16, width), bf16)
        eye = lax.broadcasted_iota(jnp.int32, (BLOCK, BLOCK), 0) == lax.broadcasted_iota(
            jnp.int32, (BLOCK, BLOCK), 1
        )

        def head(index, slot):
            rows = pl.ds(pl.multiple_of(index * HEAD_DIM, HEAD_DIM), HEAD_DIM)
            query = qkv_ref[0, 0, rows, 0:width]
            key = qkv_ref[0, 1, rows, 0:width]
            value = qkv_ref[0, 2, rows, 0:width]
            bias = spread[pl.ds(pl.multiple_of(index * 128, 128), 128), 0:width]
            left = jnp.concatenate([key, key_pad, hot], axis=0)
            right = jnp.concatenate([query, query_pad, bias], axis=0)
            own = jnp.sum(query.astype(f32) * key.astype(f32), axis=0, keepdims=True) + jnp.sum(
                bias.astype(f32) * hot.astype(f32), axis=0, keepdims=True
            )
            raw = tn(left, right)
            scores[slot, 0:width, 0:width] = raw
            for at in range(width // BLOCK):
                span = slice(at * BLOCK, (at + 1) * BLOCK)
                scores[slot, span, span] = jnp.where(eye, own[:, span], scores[slot, span, span])
            top = jnp.max(scores[slot, 0:width, 0:width], axis=0, keepdims=True)
            shifted = jnp.exp2(scores[slot, 0:width, 0:width] - top).astype(bf16)
            probs_ref[0, index, 0:width, 0:width] = shifted
            mixed = nn(jnp.concatenate([value, ones], axis=0), shifted)
            inverse = 1.0 / mixed[HEAD_DIM : HEAD_DIM + 1]
            inverse_ref[0, index, :, 0:width] = inverse
            context_ref[0, rows, 0:width] = (mixed[0:HEAD_DIM] * inverse).astype(bf16)

        def pair(step, carry):
            head(step * 2, 0)
            head(step * 2 + 1, 1)
            return carry

        lax.fori_loop(0, heads // 2, pair, 0)
        attended = tn(context_ref[0, :, 0:width], weights[3].reshape(width_model, width_model))
        hidden_ref[0:width, :] = tokens + attended + rows_ref[2:3, :]

    by_blocks(count, PAGE // BLOCK, body)


def mlp_kernel(
    counts_ref,
    place_ref,
    hidden_ref,
    cotangent_ref,
    rows_ref,
    bias_ref,
    up_ref,
    down_ref,
    out_ref,
    grad_hidden_ref,
    grad_up_ref,
    grad_down_ref,
    sums_ref,
    grad_bias_ref,
    up_total,
    down_total,
):
    page = pl.program_id(0)
    shards = up_ref.shape[0]
    place = place_ref[0]

    @pl.when(page == 0)
    def _():
        up_total[...] = jnp.zeros_like(up_total)
        down_total[...] = jnp.zeros_like(down_total)
        sums_ref[...] = jnp.zeros_like(sums_ref)
        grad_bias_ref[...] = jnp.zeros_like(grad_bias_ref)

    count = counts_ref[page]

    def body(width):
        valid = lax.broadcasted_iota(jnp.int32, (width, 1), 0) < count
        hidden = hidden_ref[0:width, :]
        xhat, inverse = norm_parts(hidden)
        low = (xhat * rows_ref[0:1, :] + rows_ref[1:2, :]).astype(bf16)
        grad_result = jnp.where(valid, cotangent_ref[0:width, :].astype(f32), 0.0)
        grad_low = grad_result.astype(bf16)

        def shard(at, carry):
            down_proj, grad_normed = carry
            upper = nn(low, up_ref[at]) + bias_ref[at]
            half = 0.5 * (1.0 + lax.erf(upper * 0.7071067811865476))
            density = jnp.exp(-0.5 * upper * upper) * 0.3989422804014327
            active = (upper * half).astype(bf16)
            slope = half + upper * density
            down_proj = down_proj + nn(active, down_ref[at])
            grad_upper = (nt(grad_low, down_ref[at]) * slope).astype(bf16)
            grad_normed = grad_normed + nt(grad_upper, up_ref[at])

            @pl.when(at == place)
            def _():
                up_total[...] += tn(low, grad_upper)
                down_total[...] += tn(active, grad_low)
                grad_bias_ref[...] += jnp.sum(grad_upper.astype(f32), axis=0, keepdims=True)

            return down_proj, grad_normed

        zero = jnp.zeros((width, hidden.shape[1]), f32)
        down_proj, grad_normed = lax.fori_loop(0, shards, shard, (zero, zero))
        result = jnp.where(valid, hidden + down_proj + rows_ref[2:3, :], 0.0)
        out_ref[0:width, :] = result.astype(bf16)
        grad_hidden = grad_result + norm_grad(grad_normed, xhat, inverse, rows_ref[0:1, :])
        grad_hidden_ref[0:width, :] = grad_hidden
        sums_ref[0:1, :] += jnp.sum(grad_normed * xhat, axis=0, keepdims=True)
        sums_ref[1:2, :] += jnp.sum(grad_normed, axis=0, keepdims=True)
        sums_ref[2:3, :] += jnp.sum(grad_hidden, axis=0, keepdims=True)
        sums_ref[3:4, :] += jnp.sum(grad_result, axis=0, keepdims=True)
        if width < PAGE:
            out_ref[width:PAGE, :] = jnp.zeros((PAGE - width, hidden.shape[1]), bf16)

    by_blocks(count, PAGE // BLOCK, body)

    @pl.when(page == pl.num_programs(0) - 1)
    def _():
        grad_up_ref[...] = up_total[...].astype(bf16)
        grad_down_ref[...] = down_total[...].astype(bf16)


def backward_kernel(
    counts_ref,
    place_ref,
    x_ref,
    meta_ref,
    rows_ref,
    grad_hidden_ref,
    qkv_ref,
    probs_ref,
    inverse_ref,
    context_ref,
    gathered_ref,
    grad_input_ref,
    grad_pack_ref,
    sums_ref,
    grad_bias_ref,
    levels_ref,
    weights,
    copy_sem,
    grad_qkv,
    grad_context,
    small_scores,
    pack_total,
):
    page = pl.program_id(0)
    place = place_ref[0]
    width_model = x_ref.shape[1]
    heads = probs_ref.shape[1]
    own = width_model // 4
    bins = 64

    @pl.when(page == 0)
    def _():
        copies = [
            pltpu.make_async_copy(gathered_ref.at[:, kind], weights.at[kind], copy_sem.at[kind])
            for kind in range(4)
        ]
        for copy in copies:
            copy.start()
        pack_total[...] = jnp.zeros_like(pack_total)
        sums_ref[...] = jnp.zeros_like(sums_ref)
        grad_bias_ref[...] = jnp.zeros_like(grad_bias_ref)
        levels_ref[...] = jnp.zeros_like(levels_ref)
        for copy in copies:
            copy.wait()

    count = counts_ref[page]

    def body(width):
        grad_hidden = grad_hidden_ref[0:width, :]
        grad_low = grad_hidden.astype(bf16)
        grad_context[:, 0:width] = nt(weights[3].reshape(width_model, width_model), grad_low)
        hot = one_hot_columns(meta_ref, width, bins)

        def head(index, slot):
            rows = pl.ds(pl.multiple_of(index * HEAD_DIM, HEAD_DIM), HEAD_DIM)
            query = qkv_ref[0, 0, rows, 0:width]
            key = qkv_ref[0, 1, rows, 0:width]
            value = qkv_ref[0, 2, rows, 0:width]
            probs = probs_ref[0, index, 0:width, 0:width]
            grad_mixed = (grad_context[rows, 0:width] * inverse_ref[0, index, :, 0:width]).astype(bf16)
            delta = jnp.sum(
                grad_mixed.astype(f32) * context_ref[0, rows, 0:width].astype(f32),
                axis=0,
                keepdims=True,
            )
            grad_probs = tn(value, grad_mixed)
            grad_scores = (probs.astype(f32) * (grad_probs - delta)).astype(bf16)
            small_scores[slot, 0:width, 0:width] = grad_scores
            grad_value = nt(grad_mixed, probs)
            grad_key = nt(query, grad_scores) * LN2
            both = nn(jnp.concatenate([key, hot], axis=0), grad_scores)
            grad_qkv[0, rows, 0:width] = (both[0:HEAD_DIM] * HEAD_DIM**-0.5).astype(bf16)
            grad_qkv[1, rows, 0:width] = grad_key.astype(bf16)
            grad_qkv[2, rows, 0:width] = grad_value.astype(bf16)
            levels_ref[index] += nt(both[HEAD_DIM:].astype(bf16), hot)

        def pair(step, carry):
            head(step * 2, 0)
            head(step * 2 + 1, 1)
            return carry

        lax.fori_loop(0, heads // 2, pair, 0)
        tokens = x_ref[0:width, :].astype(f32)
        xhat, inverse = norm_parts(tokens)
        low = (xhat * rows_ref[0:1, :] + rows_ref[1:2, :]).astype(bf16)
        mine = pl.ds(pl.multiple_of(place * own, own), own)
        stacked = jnp.concatenate([grad_qkv[kind, mine, 0:width] for kind in range(3)], axis=0)
        pack_total[0 : 3 * own, :] += nn(stacked, low)
        pack_total[3 * own :, :] += nn(context_ref[0, mine, 0:width], grad_low)
        wide = stacked.astype(f32)
        folded = wide[:, 0:BLOCK]
        for at in range(1, width // BLOCK):
            folded = folded + wide[:, at * BLOCK : (at + 1) * BLOCK]
        grad_bias_ref[...] += folded
        grad_normed = tn(grad_qkv[0, :, 0:width], weights[0].reshape(width_model, width_model))
        for kind in (1, 2):
            grad_normed = grad_normed + tn(
                grad_qkv[kind, :, 0:width], weights[kind].reshape(width_model, width_model)
            )
        grad_total = grad_hidden + norm_grad(grad_normed, xhat, inverse, rows_ref[0:1, :])
        grad_input_ref[0:width, :] = grad_total.astype(bf16)
        sums_ref[0:1, :] += jnp.sum(grad_normed * xhat, axis=0, keepdims=True)
        sums_ref[1:2, :] += jnp.sum(grad_normed, axis=0, keepdims=True)
        if width < PAGE:
            grad_input_ref[width:PAGE, :] = jnp.zeros((PAGE - width, width_model), bf16)

    by_blocks(count, PAGE // BLOCK, body)

    @pl.when(page == pl.num_programs(0) - 1)
    def _():
        grad_pack_ref[...] = pack_total[...].astype(bf16)


def toeplitz(tables):
    bins = tables.shape[-1]
    half = bins // 2
    levels = jnp.arange(bins, dtype=jnp.int32)
    offsets = jnp.clip(levels[:, None] - levels[None, :], -half, half - 1) + half
    pick = (offsets[:, :, None] == levels).astype(f32)
    full = jnp.einsum("khc,bac->khba", tables, pick, precision=lax.Precision.HIGHEST)
    zero = jnp.zeros_like(full[0])
    top = jnp.concatenate([full[0], zero], axis=2)
    bottom = jnp.concatenate([zero, full[1]], axis=2)
    return jnp.concatenate([top, bottom], axis=1)


def fold_levels(levels_grad, bins):
    half = bins // 2
    levels = jnp.arange(bins, dtype=jnp.int32)
    offsets = jnp.clip(levels[:, None] - levels[None, :], -half, half - 1) + half
    pick = (offsets[:, :, None] == levels).astype(f32)
    both = jnp.stack([levels_grad[:, 0:bins, 0:bins], levels_grad[:, bins:, bins:]])
    return jnp.einsum("khba,bac->khc", both, pick, precision=lax.Precision.HIGHEST)


def whole(shape):
    return pl.BlockSpec(shape, lambda *_: (0,) * len(shape), pipeline_mode=pl.Buffered(1))


def on_device(
    inputs,
    cotangent,
    counts,
    keep_mask,
    box_x,
    box_y,
    gain_one,
    shift_one,
    w_qkv,
    b_qv,
    w_out,
    b_out,
    gain_two,
    shift_two,
    w_up,
    b_up,
    w_down,
    b_down,
    rel_tables,
):
    rows_here, model = inputs.shape
    pages = rows_here // PAGE
    own_heads, bins = rel_tables.shape[1:]
    own = own_heads * HEAD_DIM
    shards = model // own
    heads = own_heads * shards
    hidden_units = w_up.shape[1]
    place = lax.axis_index("tensor").astype(jnp.int32).reshape(1)

    pack = jnp.concatenate([w_qkv.transpose(0, 2, 1).reshape(3 * own, model), w_out], axis=0)
    gathered = lax.all_gather(pack, "tensor").reshape(shards, 4, own, model)
    up_all = lax.all_gather(w_up, "tensor")
    down_all = lax.all_gather(w_down, "tensor")
    bias_all = lax.all_gather(b_qv, "tensor", axis=1, tiled=True)
    up_bias = lax.all_gather(b_up, "tensor").reshape(shards, 1, hidden_units)
    tables_all = lax.all_gather(rel_tables, "tensor", axis=1, tiled=True)

    toep = (toeplitz(tables_all) * LOG2E).astype(bf16).reshape(heads * 2 * bins, 2 * bins)
    meta = jnp.stack(
        [keep_mask.reshape(pages, PAGE), box_x.reshape(pages, PAGE), box_y.reshape(pages, PAGE)], axis=1
    )
    meta = jnp.pad(meta, ((0, 0), (0, 5), (0, 0)))
    rows_one = jnp.stack([gain_one, shift_one, b_out])
    rows_two = jnp.stack([gain_two, shift_two, b_down])

    page_rows = lambda: pl.BlockSpec((PAGE, model), lambda p, *_: (p, 0))
    meta_spec = pl.BlockSpec((1, 8, PAGE), lambda p, *_: (p, 0, 0))
    qkv_spec = pl.BlockSpec((1, 3, model, PAGE), lambda p, *_: (p, 0, 0, 0))
    probs_spec = pl.BlockSpec((1, heads, PAGE, PAGE), lambda p, *_: (p, 0, 0, 0))
    inverse_spec = pl.BlockSpec((1, heads, 1, PAGE), lambda p, *_: (p, 0, 0, 0))
    context_spec = pl.BlockSpec((1, model, PAGE), lambda p, *_: (p, 0, 0))
    anywhere = pl.BlockSpec(memory_space=pl.ANY)
    params = pltpu.CompilerParams(
        dimension_semantics=("arbitrary",), vmem_limit_bytes=VMEM_LIMIT
    )
    weight_scratch = [
        pltpu.VMEM((4, shards, own, model), bf16),
        pltpu.SemaphoreType.DMA((4,)),
    ]

    qkv, probs, inverse, context, hidden = pl.pallas_call(
        forward_kernel,
        out_shape=(
            jax.ShapeDtypeStruct((pages, 3, model, PAGE), bf16),
            jax.ShapeDtypeStruct((pages, heads, PAGE, PAGE), bf16),
            jax.ShapeDtypeStruct((pages, heads, 1, PAGE), f32),
            jax.ShapeDtypeStruct((pages, model, PAGE), bf16),
            jax.ShapeDtypeStruct((rows_here, model), f32),
        ),
        grid_spec=pltpu.PrefetchScalarGridSpec(
            num_scalar_prefetch=1,
            grid=(pages,),
            in_specs=[
                page_rows(),
                meta_spec,
                whole((3, model)),
                whole((model, 2)),
                whole((heads * 2 * bins, 2 * bins)),
                anywhere,
            ],
            out_specs=(qkv_spec, probs_spec, inverse_spec, context_spec, page_rows()),
            scratch_shapes=weight_scratch
            + [
                pltpu.VMEM((heads * 2 * bins, PAGE), bf16),
                pltpu.VMEM((2, PAGE, PAGE), f32),
            ],
        ),
        compiler_params=params,
        name="attention_forward",
    )(counts, inputs, meta, rows_one, bias_all.T, toep, gathered)

    out, grad_hidden, grad_up, grad_down, sums_two, grad_b_up = pl.pallas_call(
        mlp_kernel,
        out_shape=(
            jax.ShapeDtypeStruct((rows_here, model), bf16),
            jax.ShapeDtypeStruct((rows_here, model), f32),
            jax.ShapeDtypeStruct((model, hidden_units), bf16),
            jax.ShapeDtypeStruct((hidden_units, model), bf16),
            jax.ShapeDtypeStruct((8, model), f32),
            jax.ShapeDtypeStruct((1, hidden_units), f32),
        ),
        grid_spec=pltpu.PrefetchScalarGridSpec(
            num_scalar_prefetch=2,
            grid=(pages,),
            in_specs=[
                page_rows(),
                page_rows(),
                whole((3, model)),
                whole((shards, 1, hidden_units)),
                whole((shards, model, hidden_units)),
                whole((shards, hidden_units, model)),
            ],
            out_specs=(
                page_rows(),
                page_rows(),
                whole((model, hidden_units)),
                whole((hidden_units, model)),
                whole((8, model)),
                whole((1, hidden_units)),
            ),
            scratch_shapes=[
                pltpu.VMEM((model, hidden_units), f32),
                pltpu.VMEM((hidden_units, model), f32),
            ],
        ),
        compiler_params=params,
        name="feed_forward",
    )(counts, place, hidden, cotangent, rows_two, up_bias, up_all, down_all)

    grad_input, grad_pack, sums_one, grad_bias, levels_grad = pl.pallas_call(
        backward_kernel,
        out_shape=(
            jax.ShapeDtypeStruct((rows_here, model), bf16),
            jax.ShapeDtypeStruct((4 * own, model), bf16),
            jax.ShapeDtypeStruct((8, model), f32),
            jax.ShapeDtypeStruct((3 * own, BLOCK), f32),
            jax.ShapeDtypeStruct((heads, 2 * bins, 2 * bins), f32),
        ),
        grid_spec=pltpu.PrefetchScalarGridSpec(
            num_scalar_prefetch=2,
            grid=(pages,),
            in_specs=[
                page_rows(),
                meta_spec,
                whole((3, model)),
                page_rows(),
                qkv_spec,
                probs_spec,
                inverse_spec,
                context_spec,
                anywhere,
            ],
            out_specs=(
                page_rows(),
                whole((4 * own, model)),
                whole((8, model)),
                whole((3 * own, BLOCK)),
                whole((heads, 2 * bins, 2 * bins)),
            ),
            scratch_shapes=weight_scratch
            + [
                pltpu.VMEM((3, model, PAGE), bf16),
                pltpu.VMEM((model, PAGE), f32),
                pltpu.VMEM((2, PAGE, PAGE), bf16),
                pltpu.VMEM((4 * own, model), f32),
            ],
        ),
        compiler_params=params,
        name="attention_backward",
    )(counts, place, inputs, meta, rows_one, grad_hidden, qkv, probs, inverse, context, gathered)

    levels_own = lax.dynamic_slice_in_dim(levels_grad, place[0] * own_heads, own_heads, 0)
    grad_tables = fold_levels(levels_own, bins)
    bias_sums = jnp.sum(grad_bias, axis=1).reshape(3, own)
    grad_b_qv = jnp.stack([bias_sums[0], bias_sums[2]])

    big = lax.psum((grad_pack, grad_up, grad_down), "dp")
    small = lax.psum((sums_one, sums_two, grad_b_up, grad_b_qv, grad_tables), "dp")
    grad_pack, grad_up, grad_down = (part.astype(f32) for part in big)
    sums_one, sums_two, grad_b_up, grad_b_qv, grad_tables = small
    grad_w_qkv = grad_pack[0 : 3 * own].reshape(3, own, model).transpose(0, 2, 1)
    return (
        out,
        grad_input,
        grad_w_qkv,
        grad_b_qv,
        grad_pack[3 * own :],
        sums_two[2],
        sums_one[0],
        sums_one[1],
        sums_two[0],
        sums_two[1],
        grad_up,
        grad_b_up.reshape(-1),
        grad_down,
        sums_two[3],
        grad_tables,
    )


def solution(mesh):
    placed = (
        P("dp", None),
        P("dp", None),
        P("dp"),
        P("dp"),
        P("dp"),
        P("dp"),
        P(),
        P(),
        P(None, None, "tensor"),
        P(None, "tensor"),
        P("tensor", None),
        P(),
        P(),
        P(),
        P(None, "tensor"),
        P("tensor"),
        P("tensor", None),
        P(),
        P(None, "tensor", None),
    )
    return jax.shard_map(
        on_device,
        mesh=mesh,
        in_specs=placed,
        out_specs=(
            P("dp", None),
            P("dp", None),
            P(None, None, "tensor"),
            P(None, "tensor"),
            P("tensor", None),
            P(),
            P(),
            P(),
            P(),
            P(),
            P(None, "tensor"),
            P("tensor"),
            P("tensor", None),
            P(),
            P(None, "tensor", None),
        ),
        check_vma=False,
    )
```

time: 1060 us -> 510 us (0.48)
  waiting for transfers between devices: 712 us -> 228 us
  matrix products: 161 us -> 4.14 us
  Pallas kernels: 0 us -> 147 us
  blocking collectives: 27.2 us -> 99.9 us
  local copies, waits for them, and re-layouts: 74.7 us -> 8.26 us
  other arithmetic: 62.3 us -> 7.91 us
    psum x4 -> x1, waiting for transfers between devices: 711 us -> 45.3 us  [on_device(): big = lax.psum((grad_pack, grad_up, grad_down), 'dp')]
    all_gather x0 -> x3, waiting for transfers between devices: none -> 181 us  [the longest x1 89.5 us: on_device(): down_all = lax.all_gather(w_down, 'tensor')]
    pallas_call x0 -> x3, Pallas kernels: none -> 147 us  [the longest x1 56.1 us: on_device(): pl.pallas_call(mlp_kernel, out_shape=(jax.ShapeDtypeStruct((rows_here, mo...]
    dot_general x73 -> x2, matrix products: 149 us -> 4.14 us  [the longest x1 3.05 us: toeplitz(): jnp.einsum('khc,bac->khba', tables, pick, precision=lax.Precision.HIGHEST)]
    all_gather x0 -> x3, blocking collectives: none -> 41.3 us  [the longest x1 14.8 us: on_device(): tables_all = lax.all_gather(rel_tables, 'tensor', axis=1, tiled=True)]
    reduce_sum x16 -> x1, other arithmetic: 32.8 us -> 0.17 us  [on_device(): bias_sums = jnp.sum(grad_bias, axis=1).reshape(3, own)]
    psum x1, blocking collectives: 27.2 us -> 58.6 us  [on_device(): lax.psum((sums_one, sums_two, grad_b_up, grad_b_qv, grad_tables), 'dp')]
    unnamed x140 -> x40, local copies, waits for them, and re-layouts: 22.3 us -> 0.69 us
  transfers between devices with their start and end apart: 4 -> 4, of which waited for: 4 -> 4; matrix products, arithmetic and copies ran while one was open for 4% -> 2% of each run, Pallas kernels for 0% -> 8%
where the time goes in v1:
time: 510 us; the launch traced here: 509 us
  waiting for transfers between devices  228 us (45%)
  Pallas kernels  147 us (29%)
  blocking collectives  99.9 us (20%)
  between operations  14.4 us (3%)
  local copies, waits for them, and re-layouts  8.26 us (2%)
  other arithmetic  7.91 us (2%)
    all_gather x1, waiting for transfers between devices, on_device(): down_all = lax.all_gather(w_down, 'tensor')  89.5 us
    psum x1, blocking collectives, on_device(): lax.psum((sums_one, sums_two, grad_b_up, grad_b_qv, grad_tables), 'dp')  58.6 us
    pallas_call x1, Pallas kernels, on_device(): pl.pallas_call(mlp_kernel, out_shape=(jax.ShapeDtypeStruct((rows_here, mo...  56.1 us
    pallas_call x1, Pallas kernels, on_device(): pl.pallas_call(backward_kernel, out_shape=(jax.ShapeDtypeStruct((rows_her...  50.6 us
    all_gather x1, waiting for transfers between devices, on_device(): up_all = lax.all_gather(w_up, 'tensor')  49.4 us
    psum x1, waiting for transfers between devices, on_device(): big = lax.psum((grad_pack, grad_up, grad_down), 'dp')  45.3 us
    all_gather x1, waiting for transfers between devices, on_device(): gathered = lax.all_gather(pack, 'tensor').reshape(shards, 4, own, model)  42.4 us
    pallas_call x1, Pallas kernels, on_device(): pl.pallas_call(forward_kernel, out_shape=(jax.ShapeDtypeStruct((pages, 3,...  40 us
  transfers between devices with their start and end apart: 4, of which 4 were waited for; matrix products, arithmetic and copies ran while one was open for 2% of the time, Pallas kernels for 8%

profile of v1, /device:TPU:0, one launch (start us, length us, event | category | flops | bytes accessed | tf_op | source)
XLA Modules:
  0.0 509.5 jit_solution(9699156956270458078)
XLA Ops:
  7.2 2.4 pad_maximum_fusion
  9.7 0.7 all-gather.12.cloned.1.call-update
  10.5 0.7 all-gather.14.cloned.1.call-update
  11.3 14.8 %all_gather.31 = f32[2,12,64]{2,0,1:T(2,128)S(1)} all-gather(f32[2,3,64]{2,0,1:T(2,128)S(1)} %copy-done.17), channel_id=1, replica_groups=mesh['dp'=8,'tensor'=4] {'tensor'}, dimensions={1}, use_global_device_ids=true | all-gather | bytes 7680 | tf_op jit(solution)/shard_map/all_gather | solution.py:419
  26.2 3.1 fusion.2
  29.8 12.4 %all-gather.4 = f32[4,192,2]{1,2,0:T(2,128)S(1)} all-gather(f32[1,192,2]{1,2,0:T(2,128)S(1)} %bitcast.60), channel_id=1, replica_groups=mesh['dp'=8,'tensor'=4] {'tensor'}, dimensions={0}, use_global_device_ids=true | all-gather | bytes 7680 | tf_op jit(solution)/shard_map/all_gather | solution.py:417
  42.2 0.9 copy.48
  43.9 14.1 %all-gather.5.bias_ref = f32[4,1,768]{2,1,0:T(1,128)} all-gather(f32[1,1,768]{2,1,0:T(1,128)S(1)} %reshape.84), channel_id=3, replica_groups=mesh['dp'=8,'tensor'=4] {'tensor'}, dimensions={0}, use_global_device_ids=true | all-gather | bytes 15360 | tf_op jit(solution)/shard_map/all_gather | solution.py:418
  59.3 0.9 fusion.12
  60.2 42.4 %all-gather.10.cloned.1.call-done = bf16[3072,768]{1,0:T(8,128)(2,1)} async-done(((bf16[768,768]{1,0:T(8,128)(2,1)}), bf16[3072,768]{1,0:T(8,128)(2,1)}) %all-gather.10.cloned.1.call-update) | async-done | bytes 4718608 | tf_op jit(solution)/shard_map/all_gather | solution.py:414
  102.6 40.0 %attention_forward.1 = (bf16[4,3,768,512]{3,2,1,0:T(8,128)(2,1)}, bf16[4,12,512,512]{3,2,1,0:T(8,128)(2,1)}, f32[4,12,1,512]{3,2,1,0:T(1,128)}, bf16[4,768,512]{2,1,0:T(8,128)(2,1)}, f32[2048,768]{1,0:T(8,128)}) custom-call(s32[4]{0:T(128)} %counts_ref.5, bf16[2048,768]{1,0:T(8,128)(2,1)} %x_ref.3, s32[4,8,512]{2,1,0:T(8,128)} %pad.6.meta_ref, ...), custom_call_target="tpu_custom_call" | custom-call | tf_op jit(solution)/shard_map/attention_forward/pallas_call | solution.py:444
  142.7 49.4 %all-gather.12.cloned.1.call-done = bf16[3072,768]{1,0:T(8,128)(2,1)} async-done(((bf16[768,768]{1,0:T(8,128)(2,1)}), bf16[3072,768]{1,0:T(8,128)(2,1)}) %all-gather.12.cloned.1.call-update) | async-done | bytes 4718608 | tf_op jit(solution)/shard_map/all_gather | solution.py:415
  192.1 89.5 %all-gather.14.cloned.1.call-done = bf16[3072,768]{1,0:T(8,128)(2,1)} async-done(((bf16[768,768]{1,0:T(8,128)(2,1)}), bf16[3072,768]{1,0:T(8,128)(2,1)}) %all-gather.14.cloned.1.call-update) | async-done | bytes 4718608 | tf_op jit(solution)/shard_map/all_gather | solution.py:416
  281.6 56.1 %feed_forward.1 = (bf16[2048,768]{1,0:T(8,128)(2,1)}, f32[2048,768]{1,0:T(8,128)}, bf16[768,768]{1,0:T(8,128)(2,1)}, bf16[768,768]{1,0:T(8,128)(2,1)}, f32[8,768]{1,0:T(8,128)}, /*index=5*/f32[1,768]{1,0:T(1,128)}) custom-call(s32[4]{0:T(128)} %counts_ref.5, s32[1]{0:T(128)} %bitcast.place_ref, f32[2048,768]{1,0:T(8,128)} %get-tuple-element.31.hidden_ref, ...), custom_call_target="tpu_custom_call" | custom-call | tf_op jit(solution)/shard_map/feed_forward/pallas_call | solution.py:475
  337.7 50.6 %attention_backward.1 = (bf16[2048,768]{1,0:T(8,128)(2,1)}, bf16[768,768]{1,0:T(8,128)(2,1)}, f32[8,768]{1,0:T(8,128)}, f32[576,128]{1,0:T(8,128)}, f32[12,128,128]{2,1,0:T(8,128)}) custom-call(s32[4]{0:T(128)} %counts_ref.5, s32[1]{0:T(128)} %bitcast.place_ref, bf16[2048,768]{1,0:T(8,128)(2,1)} %x_ref.3, s32[4,8,512]{2,1,0:T(8,128)} %pad.6.meta_ref, ...), custom_call_target="tpu_custom_call" | custom-call | tf_op jit(solution)/shard_map/attention_backward/pallas_call | solution.py:513
  388.3 1.1 dynamic-slice_bitcast_fusion.1
  389.8 1.1 fusion.6
  390.9 58.6 %all-reduce.3 = (f32[2,192]{1,0:T(2,128)}, f32[8,768]{1,0:T(8,128)S(1)}, f32[8,768]{1,0:T(8,128)S(1)}, f32[768]{0:T(1024)}, f32[2,3,64]{2,1,0:T(4,128)S(1)}) all-reduce(f32[2,192]{1,0:T(2,128)S(1)} %pad_maximum_fusion.4, f32[8,768]{1,0:T(8,128)S(1)} %copy-done.4, ...), channel_id=1, replica_groups=mesh['dp'=8,'tensor'=4] {'dp'}, use_global_device_ids=true, to_apply=%region_2.3 | all-reduce | flops 13824 | bytes 110592 | tf_op jit(solution)/shard_map/psum | solution.py:561
  450.1 0.6 slice_reduce_fusion
  450.8 45.3 %all-reduce.7.cloned.1.call-done = (bf16[768,768]{1,0:T(8,128)(2,1)}, bf16[768,768]{1,0:T(8,128)(2,1)}, bf16[768,768]{1,0:T(8,128)(2,1)}) async-done(((bf16[768,768]{1,0:T(8,128)(2,1)}, bf16[768,768]{1,0:T(8,128)(2,1)}, bf16[768,768]{1,0:T(8,128)(2,1)}), (bf16[768,768]{1,0:T(8,128)(2,1)}, bf16[768,768]{1,0:T(8,128)(2,1)}, bf16[768,768]{1,0:T(8,128)(2,1)})) %all-reduce.7.cloned.1.call-update) | async-done | bytes 3538960 | tf_op jit(solution)/shard_map/psum | solution.py:560
  496.0 2.6 slice.66
  498.7 0.9 slice.67
  499.6 1.6 convert_element_type.21
  501.1 1.6 convert_element_type.22
  (65 shorter events, 3.7 us)
Async XLA Ops:
  7.2 95.5 %all-gather.10.cloned.1.call-start = ((), (), s32[]{:S(2)}) async-start(), calls=%async_computation | async-start | bytes 5898240 | tf_op jit(solution)/shard_map/all_gather | solution.py:414
  9.6 1.7 copy-start.17
  9.6 182.5 %all-gather.12.cloned.1.call-start = ((), (), s32[]{:S(2)}) async-start(), calls=%async_computation.1 | async-start | bytes 5898240 | tf_op jit(solution)/shard_map/all_gather | solution.py:415
  10.4 19.4 %copy-start.9 = (f32[768]{0:T(1024)S(1)}, f32[768]{0:T(1024)}, u32[]{:S(2)}) copy-start(f32[768]{0:T(1024)} %param.25) | copy-start | bytes 9220
  10.4 19.4 %copy-start.10 = (f32[768]{0:T(1024)S(1)}, f32[768]{0:T(1024)}, u32[]{:S(2)}) copy-start(f32[768]{0:T(1024)} %param.26) | copy-start | bytes 9220
  10.4 19.4 %copy-start.11 = (f32[768]{0:T(1024)S(1)}, f32[768]{0:T(1024)}, u32[]{:S(2)}) copy-start(f32[768]{0:T(1024)} %param.30) | copy-start | bytes 9220
  10.4 19.4 %copy-start.18 = (f32[2,192]{1,0:T(2,128)S(1)}, f32[2,192]{1,0:T(2,128)}, u32[]{:S(2)}) copy-start(f32[2,192]{1,0:T(2,128)} %param.28) | copy-start | bytes 4612
  10.4 32.7 %copy-start.12 = (f32[768]{0:T(1024)S(1)}, f32[768]{0:T(1024)}, u32[]{:S(2)}) copy-start(f32[768]{0:T(1024)} %param.31) | copy-start | bytes 9220
  10.4 32.7 %copy-start.13 = (f32[768]{0:T(1024)S(1)}, f32[768]{0:T(1024)}, u32[]{:S(2)}) copy-start(f32[768]{0:T(1024)} %param.32) | copy-start | bytes 9220
  10.4 32.7 %copy-start.14 = (f32[768]{0:T(1024)S(1)}, f32[768]{0:T(1024)}, u32[]{:S(2)}) copy-start(f32[768]{0:T(1024)} %param.36) | copy-start | bytes 9220
  10.4 32.7 %copy-start.15 = (f32[768]{0:T(1024)S(1)}, f32[768]{0:T(1024)}, u32[]{:S(2)}) copy-start(f32[768]{0:T(1024)} %param.34) | copy-start | bytes 9220
  10.5 32.7 %copy-start.6 = (s32[2048]{0:T(1024)S(1)}, s32[2048]{0:T(1024)}, u32[]{:S(2)}) copy-start(s32[2048]{0:T(1024)} %param.24) | copy-start | bytes 24580
  10.5 32.7 %copy-start.7 = (s32[2048]{0:T(1024)S(1)}, s32[2048]{0:T(1024)}, u32[]{:S(2)}) copy-start(s32[2048]{0:T(1024)} %param.23) | copy-start | bytes 24580
  10.5 32.7 %copy-start.8 = (s32[2048]{0:T(1024)S(1)}, s32[2048]{0:T(1024)}, u32[]{:S(2)}) copy-start(s32[2048]{0:T(1024)} %param.22) | copy-start | bytes 24580
  10.5 271.1 %all-gather.14.cloned.1.call-start = ((), (), s32[]{:S(2)}) async-start(), calls=%async_computation.2 | async-start | bytes 5898240 | tf_op jit(solution)/shard_map/all_gather | solution.py:416
  11.2 484.8 %all-reduce.7.cloned.1.call-start = ((), (), s32[]{:S(2)}) async-start(), calls=%async_computation.3 | async-start | bytes 7077888 | tf_op jit(solution)/shard_map/psum | solution.py:560
  388.2 1.4 copy-start.3
  388.2 1.5 copy-start.16
  388.3 2.7 copy-start.4
  388.3 2.6 copy-start.5
  496.0 2.7 copy-start
  496.0 3.5 copy-start.2
  498.7 2.4 copy-start.1
Sparse Core Ops, SparseCore 0:
  10.2 92.4 all-gather.9
  104.2 87.8 all-gather.11
  193.7 87.8 all-gather.13
  388.4 107.5 all-reduce.6
